TPU v7x, 256 devices: a whole 4x4x8 slice. The times are simulated.
256 devices in a mesh: ctx: 64 (over y_hi, z, x), tp: 4 (over y_lo, core).
Axes of the slice: x: 4, y: 4 (y_hi: 2, y_lo: 2; y = y_hi * 2 + y_lo), z: 8, core: 2. Of those that a mesh axis runs over, the one named last changes fastest.
Arguments:
- ids: int32 [32768], P('ctx'), may hold values from 0 to 511
- embed_table: bfloat16 [512, 4096], P(None, 'tp'), may hold values from -126 to 126
- norm_gain: float32 [4096], replicated, may hold values from 0.1 to 1.9
- in_weight: bfloat16 [3, 4096, 4096], P(None, 'ctx', 'tp'), may hold values from -0.09375 to 0.09375
- in_scale: float32 [3, 4096], P(None, 'tp'), may hold values from 0.1 to 1.9
- short_filter: float32 [3, 7, 4096], P(None, None, 'tp'), may hold values from -2.4 to 2.4
- long_filter: float32 [128, 256], P(None, 'tp'), may hold values from -0.9 to 0.9
- decay: float32 [256], P('tp'), may hold values from 0.003 to 0.1
Outputs:
- mixed: bfloat16 [32768, 4096], P('ctx', 'tp')
All inputs are finite; a program needn't handle non-finite values.
Results may differ from a plain program's by a relative error of at most 0.009.
Values may be sent and summed in bfloat16 or wider, within the bound.
No kernel may reach another device: no remote copies, remote signals or barrier semaphores. Data moves between devices by JAX's collectives and lax.ppermute only.
A program may use at most 128 MiB of HBM per device.

v0:
```python
import jax
import jax.numpy as jnp
from jax import lax
from jax.sharding import PartitionSpec as P

GROUP = 16
SHORT_TAPS = 7
LONG_TAPS = 128


def passed_along(value, axis, steps):
    count = lax.axis_size(axis)
    pairs = [(source, (source + steps) % count) for source in range(count)]
    return lax.ppermute(value, axis, pairs)


def toeplitz(long_filter, decay):
    steps = jnp.arange(LONG_TAPS, dtype=jnp.float32)
    taps = (long_filter * jnp.exp(-decay[None, :] * steps[:, None])).astype(jnp.bfloat16)
    offset = (
        jnp.arange(LONG_TAPS, dtype=jnp.int32)[:, None]
        - jnp.arange(LONG_TAPS, dtype=jnp.int32)[None, :]
    )
    lower = jnp.take(taps, jnp.clip(offset, 0, LONG_TAPS - 1), axis=0)
    upper = jnp.take(taps, jnp.clip(offset + LONG_TAPS, 0, LONG_TAPS - 1), axis=0)
    zero_tap = jnp.zeros((), jnp.bfloat16)
    toep_near = jnp.where((offset >= 0)[:, :, None], lower, zero_tap)
    toep_far = jnp.where((offset < 0)[:, :, None], upper, zero_tap)
    return (toep_near, toep_far)


def short_conv(extended, filt, out_len):
    margin = SHORT_TAPS - 1
    total = jnp.zeros((extended.shape[0], out_len, extended.shape[2]), jnp.float32)
    for k in range(SHORT_TAPS):
        window = extended[:, margin - k : margin - k + out_len, :].astype(jnp.float32)
        total = total + filt[:, k, None, :] * window
    return total


def per_device(ids, embed_table, norm_gain, in_weight, in_scale, short_filter, long_filter, decay):
    rows = ids.shape[0]
    vocab = embed_table.shape[0]
    width_local = embed_table.shape[1]
    onehot = (ids[:, None] == lax.iota(jnp.int32, vocab)[None, :]).astype(jnp.bfloat16)
    local = jnp.dot(onehot, embed_table, preferred_element_type=jnp.float32).astype(jnp.bfloat16)
    local_f = local.astype(jnp.float32)
    total = lax.psum(jnp.sum(local_f * local_f, axis=1), "tp")
    full_width = width_local * lax.axis_size("tp")
    gain = lax.dynamic_slice_in_dim(norm_gain, lax.axis_index("tp") * width_local, width_local, 0)
    scaled = local_f * lax.rsqrt(total[:, None] / full_width + 1e-06) * gain[None, :]
    features = lax.all_gather(scaled.astype(jnp.bfloat16), "tp", axis=1, tiled=True)

    def add_one(piece):
        return jnp.dot(features, piece, preferred_element_type=jnp.float32)

    def project_stream(weight):
        return add_one(lax.all_gather(weight, "ctx", axis=0, tiled=True))

    summed = jnp.stack([project_stream(in_weight[p]) for p in range(3)], axis=0)
    proj = (summed * in_scale[:, None, :]).astype(jnp.bfloat16)
    margin = SHORT_TAPS - 1
    before = passed_along(proj[:, rows - margin :, :], "ctx", 1)
    streams = short_conv(jnp.concatenate([before, proj], axis=1), short_filter, rows)
    gate = streams[0]
    inner = (streams[1] * streams[2]).astype(jnp.bfloat16)
    previous = passed_along(inner[rows - LONG_TAPS :], "ctx", 1)
    extended = jnp.concatenate([previous, inner], axis=0)
    groups_local = long_filter.shape[1]
    blocks = extended.reshape(rows // LONG_TAPS + 1, LONG_TAPS, groups_local, GROUP)
    toep_near, toep_far = toeplitz(long_filter, decay)
    conv = jnp.einsum("tsg,bsgc->btgc", toep_near, blocks[1:], preferred_element_type=jnp.float32)
    conv = conv + jnp.einsum(
        "tsg,bsgc->btgc", toep_far, blocks[:-1], preferred_element_type=jnp.float32
    )
    conv = conv.reshape(rows, width_local)
    return (gate * conv).astype(jnp.bfloat16)


def solution(mesh):
    placed = (
        P("ctx"),
        P(None, "tp"),
        P(),
        P(None, "ctx", "tp"),
        P(None, "tp"),
        P(None, None, "tp"),
        P(None, "tp"),
        P("tp"),
    )
    return jax.shard_map(
        per_device, mesh=mesh, in_specs=placed, out_specs=P("ctx", "tp"), check_vma=False
    )
```

profile of v0, /device:TPU:8, one launch (start us, length us, event | category | flops | bytes accessed | tf_op | source)
XLA Modules:
  0.0 709.9 jit_solution(41815037206658026)
XLA Ops:
  9.3 5.7 psum.7
  19.6 48.7 %all-gather.8.cloned.1.call-done = bf16[512,4096]{1,0:T(8,128)(2,1)} async-done(((bf16[512,1024]{1,0:T(8,128)(2,1)}), bf16[512,4096]{1,0:T(8,128)(2,1)}) %all-gather.8.cloned.1.call-update) | async-done | bytes 4194320 | tf_op jit(solution)/shard_map/all_gather | solution.py:52
  68.4 152.4 %all-gather.10.cloned.1.call-done = bf16[1,4096,1024]{2,1,0:T(8,128)(2,1)} async-done(((bf16[1,64,1024]{2,1,0:T(8,128)(2,1)}), bf16[1,4096,1024]{2,1,0:T(8,128)(2,1)}) %all-gather.10.cloned.1.call-update) | async-done | bytes 8388624 | tf_op jit(solution)/shard_map/all_gather | solution.py:58
  220.8 8.1 %fusion.26 = f32[1,512,1024]{2,1,0:T(8,128)S(1)} fusion(bf16[512,4096]{1,0:T(8,128)(2,1)} %all-gather.8.cloned.1.call-done, bf16[1,4096,1024]{2,1,0:T(8,128)(2,1)} %all-gather.10.cloned.1.call-done), kind=kOutput, calls=%fused_computation.47 | convolution fusion | flops 4294967296 | bytes 14680064 | tf_op jit(solution)/shard_map/dot_general | solution.py:55
  228.9 139.4 %all-gather.12.cloned.1.call-done = bf16[1,4096,1024]{2,1,0:T(8,128)(2,1)} async-done(((bf16[1,64,1024]{2,1,0:T(8,128)(2,1)}), bf16[1,4096,1024]{2,1,0:T(8,128)(2,1)}) %all-gather.12.cloned.1.call-update) | async-done | bytes 8388624 | tf_op jit(solution)/shard_map/all_gather | solution.py:58
  368.3 10.5 %fusion.29 = f32[1,512,1024]{2,1,0:T(8,128)} fusion(bf16[512,4096]{1,0:T(8,128)(2,1)} %all-gather.8.cloned.1.call-done, bf16[1,4096,1024]{2,1,0:T(8,128)(2,1)} %all-gather.12.cloned.1.call-done), kind=kOutput, calls=%fused_computation.48 | convolution fusion | flops 4294967296 | bytes 14680064 | tf_op jit(solution)/shard_map/dot_general | solution.py:55
  378.7 136.9 %all-gather.14.cloned.1.call-done = bf16[1,4096,1024]{2,1,0:T(8,128)(2,1)} async-done(((bf16[1,64,1024]{2,1,0:T(8,128)(2,1)}), bf16[1,4096,1024]{2,1,0:T(8,128)(2,1)}) %all-gather.14.cloned.1.call-update) | async-done | bytes 8388624 | tf_op jit(solution)/shard_map/all_gather | solution.py:58
  515.6 8.3 %fusion.32 = f32[1,512,1024]{2,1,0:T(8,128)S(1)} fusion(bf16[512,4096]{1,0:T(8,128)(2,1)} %all-gather.8.cloned.1.call-done, bf16[1,4096,1024]{2,1,0:T(8,128)(2,1)} %all-gather.14.cloned.1.call-done), kind=kOutput, calls=%fused_computation.49 | convolution fusion | flops 4294967296 | bytes 14680064 | tf_op jit(solution)/shard_map/dot_general | solution.py:55
  524.9 1.7 copy-done.3
  526.6 1.7 collective-permute-start
  528.3 57.8 %gather_fusion.1 = bf16[16384,64]{1,0:T(8,128)(2,1)} fusion(bf16[128,64]{1,0:T(8,128)(2,1)S(1)} %multiply_convert_fusion, s32[16384]{0:T(1024)S(1)} %bitcast_clamp_fusion), kind=kCustom, calls=%fused_computation.1.clone | custom fusion | bytes 4259840 | tf_op jit(solution)/shard_map/jit(_take)/gather | solution.py:25
  586.2 5.7 copy.20
  591.9 57.8 %gather_fusion = bf16[16384,64]{1,0:T(8,128)(2,1)} fusion(bf16[128,64]{1,0:T(8,128)(2,1)S(1)} %multiply_convert_fusion, s32[16384]{0:T(1024)S(1)} %bitcast_clamp_fusion.1), kind=kCustom, calls=%fused_computation.clone | custom fusion | bytes 4259840 | tf_op jit(solution)/shard_map/jit(_take)/gather | solution.py:24
  649.7 4.8 copy.17
  654.5 13.6 %multiply_add_fusion = f32[3,512,1024]{2,1,0:T(8,128)S(1)} fusion(bf16[3,512,1024]{2,1,0:T(8,128)(2,1)} %copy-done.3, bf16[3,6,1024]{2,1,0:T(8,128)(2,1)S(1)} %collective-permute-done, f32[3,1024]{1,0:T(4,128)S(1)} %get-tuple-element.18, f32[3,1024]{1,0:T(4,128)S(1)} %get-tuple-element.19, f32[3,1024]{1,0:T(4,128)S(1)} %get-tuple-element.20, ...), kind=kLoop, calls=%fused_computation.15 | loop fusion | flops 59768832 | bytes 9560064 | tf_op jit(solution)/shard_map/add | solution.py:37
  668.1 2.6 copy-done.2
  675.9 2.5 fusion.62
  678.5 6.9 collective-permute-done.1
  686.5 2.3 copy.19
  688.7 2.1 slice.97
  690.9 3.5 fusion.18
  694.3 1.6 add_bitcast_fusion
  698.5 2.0 copy.23
  700.5 2.9 fusion.17
  (54 shorter events, 17.0 us)
Async XLA Ops:
  6.5 1.2 copy-start
  6.5 10.5 %copy-start.5 = (bf16[3,64,1024]{2,1,0:T(8,128)(2,1)S(1)}, bf16[3,64,1024]{2,1,0:T(8,128)(2,1)}, u32[]{:S(2)}) copy-start(bf16[3,64,1024]{2,1,0:T(8,128)(2,1)} %param.13) | copy-start | bytes 1179652
  6.5 12.7 %copy-start.7 = (f32[128,64]{0,1:T(8,128)S(1)}, f32[128,64]{0,1:T(8,128)}, u32[]{:S(2)}) copy-start(f32[128,64]{0,1:T(8,128)} %param.16) | copy-start | bytes 98308
  6.5 12.8 %copy-start.9 = (f32[64]{0:T(128)S(1)}, f32[64]{0:T(128)}, u32[]{:S(2)}) copy-start(f32[64]{0:T(128)} %param.17) | copy-start | bytes 772
  6.5 12.9 %copy-start.6 = (f32[3,7,1024]{2,1,0:T(8,128)S(1)}, f32[3,7,1024]{2,1,0:T(8,128)}, u32[]{:S(2)}) copy-start(f32[3,7,1024]{2,1,0:T(8,128)} %param.15) | copy-start | bytes 258052
  6.5 61.8 %all-gather.8.cloned.1.call-start = ((), (), s32[]{:S(2)}) async-start(), calls=%async_computation | async-start | bytes 5242880 | tf_op jit(solution)/shard_map/all_gather | solution.py:52
  17.0 203.7 %all-gather.10.cloned.1.call-start = ((), (), s32[]{:S(2)}) async-start(), calls=%async_computation.1 | async-start | bytes 8519680 | tf_op jit(solution)/shard_map/all_gather | solution.py:58
  17.9 350.4 %all-gather.12.cloned.1.call-start = ((), (), s32[]{:S(2)}) async-start(), calls=%async_computation.2 | async-start | bytes 8519680 | tf_op jit(solution)/shard_map/all_gather | solution.py:58
  18.6 497.0 %all-gather.14.cloned.1.call-start = ((), (), s32[]{:S(2)}) async-start(), calls=%async_computation.3 | async-start | bytes 8519680 | tf_op jit(solution)/shard_map/all_gather | solution.py:58
  378.7 145.2 %copy-start.8 = (f32[3,1024]{1,0:T(4,128)S(1)}, f32[3,1024]{1,0:T(4,128)}, u32[]{:S(2)}) copy-start(f32[3,1024]{1,0:T(4,128)} %param.14) | copy-start | bytes 36868
  515.6 8.3 %copy-start.4 = (f32[1,512,1024]{2,1,0:T(8,128)S(1)}, f32[1,512,1024]{2,1,0:T(8,128)}, u32[]{:S(2)}) copy-start(f32[1,512,1024]{2,1,0:T(8,128)} %fusion.29) | copy-start | bytes 6291460
  524.9 1.7 copy-start.3
  526.6 128.0 %collective-permute-start = (bf16[3,6,1024]{2,1,0:T(8,128)(2,1)S(1)}, bf16[3,6,1024]{2,1,0:T(8,128)(2,1)S(1)}, u32[]{:S(2)}, u32[]{:S(2)}) collective-permute-start(bf16[3,6,1024]{2,1,0:T(8,128)(2,1)S(1)} %slice.102), channel_id=1, source_target_pairs={{0,4},{4,8},{8,12},{12,16},{16,20},{20,24},{24,28},{28,32},{32,36}... | collective-permute-start | bytes 110600 | tf_op jit(solution)/shard_map/ppermute | solution.py:14
  668.1 2.7 copy-start.2
  673.1 12.3 %collective-permute-start.1 = (bf16[128,1024]{1,0:T(8,128)(2,1)}, bf16[128,1024]{1,0:T(8,128)(2,1)S(1)}, u32[]{:S(2)}, u32[]{:S(2)}) collective-permute-start(bf16[128,1024]{1,0:T(8,128)(2,1)} %slice_bitcast_fusion.1), channel_id=1, source_target_pairs={{0,4},{4,8},{8,12},{12,16},{16,20},{20,24},{24,28},{28,32},{32,36}... | collective-permute-start | bytes 786440 | tf_op jit(solution)/shard_map/ppermute | solution.py:14
  698.5 4.9 copy-start.1
Sparse Core Ops, SparseCore 0:
  17.1 51.1 all-gather.7
  71.9 148.8 all-gather.9
  224.2 143.9 all-gather.11
  371.6 143.9 all-gather.13
where the time goes:
time: 710 us
  waiting for transfers between devices  486 us (68%)
  local copies, waits for them, and re-layouts  146 us (21%)
  matrix products  33.5 us (5%)
  other arithmetic  22.8 us (3%)
  between operations  13.4 us (2%)
    all_gather x3, waiting for transfers between devices, project_stream(): return add_one(lax.all_gather(weight, 'ctx', axis=0, tiled=True))  429 us
    gather x2, local copies, waits for them, and re-layouts, toeplitz(): jnp.take(taps, jnp.clip(offset + LONG_TAPS, 0, LONG_TAPS - 1), axis=0)  63.5 us
    gather x2, local copies, waits for them, and re-layouts, toeplitz(): lower = jnp.take(taps, jnp.clip(offset, 0, LONG_TAPS - 1), axis=0)  62.6 us
    all_gather x1, waiting for transfers between devices, per_device(): lax.all_gather(scaled.astype(jnp.bfloat16), 'tp', axis=1, tiled=True)  48.7 us
    dot_general x3, matrix products, add_one(): return jnp.dot(features, piece, preferred_element_type=jnp.float32)  26.9 us
  transfers between devices with their start and end apart: 6, of which 5 were waited for; matrix products, arithmetic and copies ran while one was open for 21% of the time, Pallas kernels for 0%

commit v1 on v0

--- a/solution.py
+++ b/solution.py
@@ -49,7 +49,9 @@
     full_width = width_local * lax.axis_size("tp")
     gain = lax.dynamic_slice_in_dim(norm_gain, lax.axis_index("tp") * width_local, width_local, 0)
     scaled = local_f * lax.rsqrt(total[:, None] / full_width + 1e-06) * gain[None, :]
-    features = lax.all_gather(scaled.astype(jnp.bfloat16), "tp", axis=1, tiled=True)
+    block = scaled.astype(jnp.bfloat16)
+    stack = jnp.stack([block] * lax.axis_size("tp"))
+    features = jnp.concatenate(lax.all_to_all(stack, "tp", 0, 0), axis=1)
 
     def add_one(piece):
         return jnp.dot(features, piece, preferred_element_type=jnp.float32)

time: 710 us -> 653 us (0.920)
  waiting for transfers between devices: 486 us -> 419 us
  starting transfers between devices: 3.36 us -> 10.5 us
    all_gather x3, waiting for transfers between devices: 429 us -> 360 us  [project_stream(): return add_one(lax.all_gather(weight, 'ctx', axis=0, tiled=True))]
    all_to_all x0 -> x1, waiting for transfers between devices: none -> 50.1 us  [per_device(): features = jnp.concatenate(lax.all_to_all(stack, 'tp', 0, 0), axis=1)]
    all_gather x1 -> x0, waiting for transfers between devices: 48.7 us -> none  [per_device(): lax.all_gather(scaled.astype(jnp.bfloat16), 'tp', axis=1, tiled=True)]
    all_to_all x0 -> x1, starting transfers between devices: none -> 7.23 us  [per_device(): features = jnp.concatenate(lax.all_to_all(stack, 'tp', 0, 0), axis=1)]
  transfers between devices with their start and end apart: 6 -> 6, of which waited for: 5 -> 5; matrix products, arithmetic and copies ran while one was open for 21% -> 24% of each run, Pallas kernels for 0% -> 0%
where the time goes in v1:
time: 653 us; the launch traced here: 652 us
  waiting for transfers between devices  419 us (64%)
  local copies, waits for them, and re-layouts  148 us (23%)
  matrix products  33.6 us (5%)
  other arithmetic  22 us (3%)
  between operations  13.4 us (2%)
  starting transfers between devices  10.5 us (2%)
    all_gather x3, waiting for transfers between devices, project_stream(): return add_one(lax.all_gather(weight, 'ctx', axis=0, tiled=True))  360 us
    gather x2, local copies, waits for them, and re-layouts, toeplitz(): jnp.take(taps, jnp.clip(offset + LONG_TAPS, 0, LONG_TAPS - 1), axis=0)  63.5 us
    gather x2, local copies, waits for them, and re-layouts, toeplitz(): lower = jnp.take(taps, jnp.clip(offset, 0, LONG_TAPS - 1), axis=0)  62.6 us
    all_to_all x1, waiting for transfers between devices, per_device(): features = jnp.concatenate(lax.all_to_all(stack, 'tp', 0, 0), axis=1)  50.1 us
    dot_general x3, matrix products, add_one(): return jnp.dot(features, piece, preferred_element_type=jnp.float32)  27 us
    add x1, other arithmetic, short_conv(): total = total + filt[:, k, None, :] * window  13.8 us
  transfers between devices with their start and end apart: 6, of which 5 were waited for; matrix products, arithmetic and copies ran while one was open for 24% of the time, Pallas kernels for 0%

profile of v1, /device:TPU:8, one launch (start us, length us, event | category | flops | bytes accessed | tf_op | source)
XLA Modules:
  0.0 652.3 jit_solution(14368022871548475634)
XLA Ops:
  6.5 1.9 fusion.56
  12.1 5.7 psum.7
  18.7 2.3 stack.19
  21.0 7.2 %all-to-all-start = ((bf16[4,512,1024]{1,2,0:T(8,128)(2,1)}), bf16[4,512,1024]{1,2,0:T(8,128)(2,1)}, u32[]{:S(2)}, u32[]{:S(2)}) async-start(bf16[4,512,1024]{1,2,0:T(8,128)(2,1)} %stack.19), calls=%async_computation | async-start | bytes 8388608 | tf_op jit(solution)/shard_map/all_to_all | solution.py:54
  28.7 50.1 %all-to-all-done = bf16[4,512,1024]{1,2,0:T(8,128)(2,1)} async-done(((bf16[4,512,1024]{1,2,0:T(8,128)(2,1)}), bf16[4,512,1024]{1,2,0:T(8,128)(2,1)}, u32[]{:S(2)}, u32[]{:S(2)}) %all-to-all-start) | async-done | bytes 4194336 | tf_op jit(solution)/shard_map/all_to_all | solution.py:54
  78.7 84.0 %all-gather.7.cloned.1.call-done = bf16[1,4096,1024]{2,1,0:T(8,128)(2,1)} async-done(((bf16[1,64,1024]{2,1,0:T(8,128)(2,1)}), bf16[1,4096,1024]{2,1,0:T(8,128)(2,1)}) %all-gather.7.cloned.1.call-update) | async-done | bytes 8388624 | tf_op jit(solution)/shard_map/all_gather | solution.py:60
  162.8 8.2 %fusion.26 = f32[1,512,1024]{2,1,0:T(8,128)S(1)} fusion(bf16[512,4096]{0,1:T(8,128)(2,1)} %bitcast.1, bf16[1,4096,1024]{2,1,0:T(8,128)(2,1)} %all-gather.7.cloned.1.call-done), kind=kOutput, calls=%fused_computation.47 | convolution fusion | flops 4294967296 | bytes 14680064 | tf_op jit(solution)/shard_map/dot_general | solution.py:57
  171.0 139.3 %all-gather.9.cloned.1.call-done = bf16[1,4096,1024]{2,1,0:T(8,128)(2,1)} async-done(((bf16[1,64,1024]{2,1,0:T(8,128)(2,1)}), bf16[1,4096,1024]{2,1,0:T(8,128)(2,1)}) %all-gather.9.cloned.1.call-update) | async-done | bytes 8388624 | tf_op jit(solution)/shard_map/all_gather | solution.py:60
  310.2 10.5 %fusion.29 = f32[1,512,1024]{2,1,0:T(8,128)} fusion(bf16[512,4096]{0,1:T(8,128)(2,1)} %bitcast.1, bf16[1,4096,1024]{2,1,0:T(8,128)(2,1)} %all-gather.9.cloned.1.call-done), kind=kOutput, calls=%fused_computation.48 | convolution fusion | flops 4294967296 | bytes 14680064 | tf_op jit(solution)/shard_map/dot_general | solution.py:57
  320.8 137.0 %all-gather.11.cloned.1.call-done = bf16[1,4096,1024]{2,1,0:T(8,128)(2,1)} async-done(((bf16[1,64,1024]{2,1,0:T(8,128)(2,1)}), bf16[1,4096,1024]{2,1,0:T(8,128)(2,1)}) %all-gather.11.cloned.1.call-update) | async-done | bytes 8388624 | tf_op jit(solution)/shard_map/all_gather | solution.py:60
  457.8 8.3 %fusion.32 = f32[1,512,1024]{2,1,0:T(8,128)S(1)} fusion(bf16[512,4096]{0,1:T(8,128)(2,1)} %bitcast.1, bf16[1,4096,1024]{2,1,0:T(8,128)(2,1)} %all-gather.11.cloned.1.call-done), kind=kOutput, calls=%fused_computation.49 | convolution fusion | flops 4294967296 | bytes 14680064 | tf_op jit(solution)/shard_map/dot_general | solution.py:57
  470.6 57.8 %gather_fusion.1 = bf16[16384,64]{1,0:T(8,128)(2,1)} fusion(bf16[128,64]{1,0:T(8,128)(2,1)S(1)} %multiply_convert_fusion, s32[16384]{0:T(1024)S(1)} %bitcast_clamp_fusion), kind=kCustom, calls=%fused_computation.1.clone | custom fusion | bytes 4259840 | tf_op jit(solution)/shard_map/jit(_take)/gather | solution.py:25
  528.4 5.7 copy.21
  534.1 57.8 %gather_fusion = bf16[16384,64]{1,0:T(8,128)(2,1)} fusion(bf16[128,64]{1,0:T(8,128)(2,1)S(1)} %multiply_convert_fusion, s32[16384]{0:T(1024)S(1)} %bitcast_clamp_fusion.1), kind=kCustom, calls=%fused_computation.clone | custom fusion | bytes 4259840 | tf_op jit(solution)/shard_map/jit(_take)/gather | solution.py:24
  591.9 4.8 copy.18
  596.7 13.8 %multiply_add_fusion = f32[3,512,1024]{2,1,0:T(8,128)S(1)} fusion(bf16[3,512,1024]{2,1,0:T(8,128)(2,1)} %copy-done.3, bf16[3,6,1024]{2,1,0:T(8,128)(2,1)S(1)} %collective-permute-done, f32[3,1024]{1,0:T(4,128)S(1)} %get-tuple-element.18, f32[3,1024]{1,0:T(4,128)S(1)} %get-tuple-element.19, f32[3,1024]{1,0:T(4,128)S(1)} %get-tuple-element.20, ...), kind=kLoop, calls=%fused_computation.15 | loop fusion | flops 59768832 | bytes 9560064 | tf_op jit(solution)/shard_map/add | solution.py:37
  610.5 2.7 copy-done.2
  618.4 2.5 fusion.62
  620.9 6.9 %collective-permute-done.1 = bf16[128,1024]{1,0:T(8,128)(2,1)S(1)} collective-permute-done((bf16[128,1024]{1,0:T(8,128)(2,1)}, bf16[128,1024]{1,0:T(8,128)(2,1)S(1)}, u32[]{:S(2)}, u32[]{:S(2)}) %collective-permute-start.1) | collective-permute-done | bytes 262176 | tf_op jit(solution)/shard_map/ppermute | solution.py:14
  628.9 2.3 copy.20
  631.2 2.1 slice.97
  633.3 3.5 fusion.18
  640.9 2.0 copy.24
  642.9 2.9 fusion.17
  (53 shorter events, 19.6 us)
Async XLA Ops:
  6.5 4.1 copy-start
  6.5 156.2 %all-gather.7.cloned.1.call-start = ((), (), s32[]{:S(2)}) async-start(), calls=%async_computation.1 | async-start | bytes 8519680 | tf_op jit(solution)/shard_map/all_gather | solution.py:60
  8.4 301.8 %all-gather.9.cloned.1.call-start = ((), (), s32[]{:S(2)}) async-start(), calls=%async_computation.2 | async-start | bytes 8519680 | tf_op jit(solution)/shard_map/all_gather | solution.py:60
  9.2 448.6 %all-gather.11.cloned.1.call-start = ((), (), s32[]{:S(2)}) async-start(), calls=%async_computation.3 | async-start | bytes 8519680 | tf_op jit(solution)/shard_map/all_gather | solution.py:60
  21.0 7.2 %copy-start.6 = (f32[128,64]{0,1:T(8,128)S(1)}, f32[128,64]{0,1:T(8,128)}, u32[]{:S(2)}) copy-start(f32[128,64]{0,1:T(8,128)} %param.16) | copy-start | bytes 98308
  21.0 7.3 %copy-start.8 = (f32[64]{0:T(128)S(1)}, f32[64]{0:T(128)}, u32[]{:S(2)}) copy-start(f32[64]{0:T(128)} %param.17) | copy-start | bytes 772
  21.0 7.5 %copy-start.5 = (f32[3,7,1024]{2,1,0:T(8,128)S(1)}, f32[3,7,1024]{2,1,0:T(8,128)}, u32[]{:S(2)}) copy-start(f32[3,7,1024]{2,1,0:T(8,128)} %param.15) | copy-start | bytes 258052
  21.0 57.7 %all-to-all-start = ((bf16[4,512,1024]{1,2,0:T(8,128)(2,1)}), bf16[4,512,1024]{1,2,0:T(8,128)(2,1)}, u32[]{:S(2)}, u32[]{:S(2)}) async-start(bf16[4,512,1024]{1,2,0:T(8,128)(2,1)} %stack.19), calls=%async_computation | async-start | bytes 8388608 | tf_op jit(solution)/shard_map/all_to_all | solution.py:54
  320.7 145.4 %copy-start.7 = (f32[3,1024]{1,0:T(4,128)S(1)}, f32[3,1024]{1,0:T(4,128)}, u32[]{:S(2)}) copy-start(f32[3,1024]{1,0:T(4,128)} %param.14) | copy-start | bytes 36868
  457.8 8.4 %copy-start.4 = (f32[1,512,1024]{2,1,0:T(8,128)S(1)}, f32[1,512,1024]{2,1,0:T(8,128)}, u32[]{:S(2)}) copy-start(f32[1,512,1024]{2,1,0:T(8,128)} %fusion.29) | copy-start | bytes 6291460
  467.1 1.7 copy-start.3
  468.8 127.9 %collective-permute-start = (bf16[3,6,1024]{2,1,0:T(8,128)(2,1)S(1)}, bf16[3,6,1024]{2,1,0:T(8,128)(2,1)S(1)}, u32[]{:S(2)}, u32[]{:S(2)}) collective-permute-start(bf16[3,6,1024]{2,1,0:T(8,128)(2,1)S(1)} %slice.102), channel_id=1, source_target_pairs={{0,4},{4,8},{8,12},{12,16},{16,20},{20,24},{24,28},{28,32},{32,36}... | collective-permute-start | bytes 110600 | tf_op jit(solution)/shard_map/ppermute | solution.py:14
  610.5 2.7 copy-start.2
  615.5 12.3 %collective-permute-start.1 = (bf16[128,1024]{1,0:T(8,128)(2,1)}, bf16[128,1024]{1,0:T(8,128)(2,1)S(1)}, u32[]{:S(2)}, u32[]{:S(2)}) collective-permute-start(bf16[128,1024]{1,0:T(8,128)(2,1)} %slice_bitcast_fusion.1), channel_id=1, source_target_pairs={{0,4},{4,8},{8,12},{12,16},{16,20},{20,24},{24,28},{28,32},{32,36}... | collective-permute-start | bytes 786440 | tf_op jit(solution)/shard_map/ppermute | solution.py:14
  640.9 4.9 copy-start.1
Sparse Core Ops, SparseCore 0:
  10.8 151.8 all-gather.6
  166.2 143.9 all-gather.8
  313.7 143.9 all-gather.10
